TPU v7x, 128 devices: a whole 4x4x4 slice. The times are simulated.
128 devices in a mesh: depth: 4 (over x), panel: 32 (over y, z, core).
Axes of the slice: x: 4, y: 4, z: 4, core: 2. Of those that a mesh axis runs over, the one named last changes fastest.
Arguments:
- diag_blocks: float32 [4, 1024, 1024], P('depth', 'panel'), as said below
- coupling: float32 [4, 1024, 1024], P('depth', 'panel'), may hold values from -0.078125 to 0.078125
- sources: float32 [4, 1024, 256], P('depth', 'panel'), may hold values from -6 to 6
- requests: int32 [4, 128], P('depth', 'panel'), may hold values from 0 to 1023, as said below
Outputs:
- panels: float32 [4, 1024, 256], P('depth', 'panel')
- picked: float32 [4, 128, 256], P('depth', 'panel')
Inputs may be any that keep to these rules, and one draw needn't show every extreme that they name: `requests`: row numbers within their block; both 0 and 1023 occur. `diag_blocks`: every diagonal block is exactly symmetric with a positive diagonal.
All inputs are finite; a program needn't handle non-finite values.
Results may differ from a plain program's by a relative error of at most 0.0001.
Values sent between devices are 32-bit elements; how exact they have to be, the bound alone decides.
No kernel may reach another device: no remote copies, remote signals or barrier semaphores. Data moves between devices by JAX's collectives and lax.ppermute only.
A program may use at most 64 MiB of HBM per device.

v0:
```python
import jax
import jax.numpy as jnp
from jax import lax
from jax.sharding import PartitionSpec as P

ITERS = 2
highest = lax.Precision.HIGHEST


def passed_along(block, axis, distance):
    devices = range(lax.axis_size(axis))
    route = [(i - distance, i) for i in devices if i - distance in devices]
    return lax.ppermute(block, axis, route)


def product_rows(matrix, panel_rows):
    initial = jnp.zeros((matrix.shape[0], panel_rows.shape[1]), jnp.float32)
    shard_rows = lax.all_gather(panel_rows, "panel", axis=0, tiled=True)
    columns = lax.slice_in_dim(matrix, 0, shard_rows.shape[0], axis=1)
    return initial + jnp.dot(
        columns, shard_rows, precision=highest, preferred_element_type=jnp.float32
    )


def product_transposed(matrix, panel_rows):
    return lax.psum_scatter(
        lax.dot_general(
            matrix,
            panel_rows,
            (((0,), (0,)), ((), ())),
            precision=highest,
            preferred_element_type=jnp.float32,
        ),
        "panel",
        scatter_dimension=0,
        tiled=True,
    )


def jacobi(matrix, diag_part, right_hand):
    scaled = diag_part[:, None]
    iterate = right_hand / scaled
    for sweep_no in range(ITERS):
        image = product_rows(matrix, iterate)
        iterate = iterate + (right_hand - image) / scaled
    return iterate


def per_device(diag_blocks, coupling, sources, requests):
    depth_count = lax.axis_size("depth")
    depth_pos = lax.axis_index("depth")
    panel_pos = lax.axis_index("panel")
    block_count = diag_blocks.shape[0]
    row_count = diag_blocks.shape[1]
    local_cols = sources.shape[2]
    own_square = lax.dynamic_slice_in_dim(diag_blocks, panel_pos * row_count, row_count, 2)
    diag_part = jnp.diagonal(own_square, axis1=1, axis2=2)
    col_groups = 1
    col_width = local_cols // col_groups
    section_total = depth_count + col_groups - 1
    left_terms = jnp.zeros_like(sources)
    carried = jnp.zeros((row_count, col_width), jnp.float32)
    for section_no in range(section_total):
        column_pos = section_no - depth_pos
        active = (column_pos >= 0) & (column_pos < col_groups)
        col_start = jnp.clip(column_pos, 0, col_groups - 1) * col_width
        block_no = 0
        source_cols = sources[block_no]
        stored = lax.dynamic_update_slice_in_dim(left_terms[block_no], carried, col_start, 1)
        left_terms = left_terms.at[block_no].set(jnp.where(active, stored, left_terms[block_no]))
        forward = jacobi(diag_blocks[block_no], diag_part[block_no], source_cols - carried)
        carried = product_transposed(coupling[block_no], forward)
        carried = passed_along(carried, "depth", 1)
    panels = jnp.zeros_like(sources)
    ahead = jnp.zeros((row_count, col_width), jnp.float32)
    for section_no in range(section_total):
        column_pos = section_no - (depth_count - 1 - depth_pos)
        active = (column_pos >= 0) & (column_pos < col_groups)
        col_start = jnp.clip(column_pos, 0, col_groups - 1) * col_width
        for block_no in reversed(range(block_count)):
            source_cols = sources[block_no]
            left_cols = left_terms[block_no]
            right_term = product_rows(coupling[block_no], ahead)
            ahead = jacobi(
                diag_blocks[block_no], diag_part[block_no], source_cols - left_cols - right_term
            )
            stored = lax.dynamic_update_slice_in_dim(panels[block_no], ahead, col_start, 1)
            panels = panels.at[block_no].set(jnp.where(active, stored, panels[block_no]))
        ahead = passed_along(ahead, "depth", -1)
    picked_rows = requests.shape[1]
    shard_rows = lax.all_gather(panels, "panel", axis=1, tiled=True)
    shard_len = shard_rows.shape[1]
    inside = (requests >= 0) & (requests < shard_len)
    clipped = jnp.clip(requests, 0, shard_len - 1)
    where_rows = jnp.broadcast_to(
        clipped[:, :, None], (block_count, picked_rows, shard_rows.shape[2])
    )
    taken = jnp.take_along_axis(shard_rows, where_rows, axis=1)
    picked = jnp.where(inside[:, :, None], taken, 0.0)
    return (panels, picked)


def solution(mesh):
    placed = (
        P("depth", "panel", None),
        P("depth", "panel", None),
        P("depth", "panel", None),
        P("depth", "panel"),
    )
    return jax.shard_map(
        per_device,
        mesh=mesh,
        in_specs=placed,
        out_specs=(P("depth", "panel", None), P("depth", "panel", None)),
        check_vma=False,
    )
```

profile of v0, /device:TPU:1, one launch (start us, length us, event | category | flops | bytes accessed | tf_op | source)
XLA Modules:
  0.0 1144.0 jit_solution(601774973997432605)
XLA Ops:
  7.2 0.8 copy-done
  8.2 0.7 gather_fusion
  8.9 0.7 bitcast_divide_fusion
  9.7 47.5 %all-gather.20.cloned.1.call-done = f32[1024,256]{1,0:T(8,128)} async-done(((f32[32,256]{1,0:T(8,128)}), f32[1024,256]{1,0:T(8,128)}) %all-gather.20.cloned.1.call-update) | async-done | bytes 1048592 | tf_op jit(solution)/shard_map/all_gather | solution.py:18
  57.1 2.5 fusion.45
  59.7 42.2 %all-gather.22.cloned.1.call-done = f32[1024,256]{1,0:T(8,128)} async-done(((f32[32,256]{1,0:T(8,128)}), f32[1024,256]{1,0:T(8,128)}) %all-gather.22.cloned.1.call-update) | async-done | bytes 1048592 | tf_op jit(solution)/shard_map/all_gather | solution.py:18
  102.0 1.9 fusion.42
  103.8 2.0 convolution_bitcast_fusion.2
  105.9 75.1 %reduce-scatter.4.cloned.1.call-done = f32[32,256]{1,0:T(8,128)} async-done(((f32[1024,256]{1,0:T(8,128)}), f32[32,256]{1,0:T(8,128)}) %reduce-scatter.4.cloned.1.call-update) | async-done | bytes 32784 | tf_op jit(solution)/shard_map/reduce_scatter | solution.py:26
  181.1 3.1 collective-permute-start
  184.2 1.3 collective-permute-done
  185.5 0.7 broadcast_divide_fusion.4
  186.2 45.9 %all-gather.24.cloned.1.call-done = f32[1024,256]{1,0:T(8,128)} async-done(((f32[32,256]{1,0:T(8,128)}), f32[1024,256]{1,0:T(8,128)}) %all-gather.24.cloned.1.call-update) | async-done | bytes 1048592 | tf_op jit(solution)/shard_map/all_gather | solution.py:18
  232.1 2.5 fusion.39
  234.7 42.1 %all-gather.26.cloned.1.call-done = f32[1024,256]{1,0:T(8,128)} async-done(((f32[32,256]{1,0:T(8,128)}), f32[1024,256]{1,0:T(8,128)}) %all-gather.26.cloned.1.call-update) | async-done | bytes 1048592 | tf_op jit(solution)/shard_map/all_gather | solution.py:18
  276.8 1.9 fusion.36
  278.7 2.0 convolution_bitcast_fusion.1
  280.8 75.1 %reduce-scatter.6.cloned.1.call-done = f32[32,256]{1,0:T(8,128)} async-done(((f32[1024,256]{1,0:T(8,128)}), f32[32,256]{1,0:T(8,128)}) %reduce-scatter.6.cloned.1.call-update) | async-done | bytes 32784 | tf_op jit(solution)/shard_map/reduce_scatter | solution.py:26
  355.9 3.1 collective-permute-start.1
  359.0 1.3 collective-permute-done.1
  360.3 0.7 broadcast_divide_fusion.3
  361.0 45.9 %all-gather.28.cloned.1.call-done = f32[1024,256]{1,0:T(8,128)} async-done(((f32[32,256]{1,0:T(8,128)}), f32[1024,256]{1,0:T(8,128)}) %all-gather.28.cloned.1.call-update) | async-done | bytes 1048592 | tf_op jit(solution)/shard_map/all_gather | solution.py:18
  406.9 2.5 fusion.33
  409.5 42.2 %all-gather.30.cloned.1.call-done = f32[1024,256]{1,0:T(8,128)} async-done(((f32[32,256]{1,0:T(8,128)}), f32[1024,256]{1,0:T(8,128)}) %all-gather.30.cloned.1.call-update) | async-done | bytes 1048592 | tf_op jit(solution)/shard_map/all_gather | solution.py:18
  451.8 1.9 fusion.30
  453.6 2.0 convolution_bitcast_fusion
  455.7 75.1 %reduce-scatter.8.cloned.1.call-done = f32[32,256]{1,0:T(8,128)} async-done(((f32[1024,256]{1,0:T(8,128)}), f32[32,256]{1,0:T(8,128)}) %reduce-scatter.8.cloned.1.call-update) | async-done | bytes 32784 | tf_op jit(solution)/shard_map/reduce_scatter | solution.py:26
  530.9 3.1 collective-permute-start.2
  534.1 1.2 collective-permute-done.2
  535.3 0.7 subtract_divide_fusion
  536.0 45.9 %all-gather.32.cloned.1.call-done = f32[1024,256]{1,0:T(8,128)} async-done(((f32[32,256]{1,0:T(8,128)}), f32[1024,256]{1,0:T(8,128)}) %all-gather.32.cloned.1.call-update) | async-done | bytes 1048592 | tf_op jit(solution)/shard_map/all_gather | solution.py:18
  581.9 2.5 fusion.27
  584.5 42.3 %all-gather.34.cloned.1.call-done = f32[1024,256]{1,0:T(8,128)} async-done(((f32[32,256]{1,0:T(8,128)}), f32[1024,256]{1,0:T(8,128)}) %all-gather.34.cloned.1.call-update) | async-done | bytes 1048592 | tf_op jit(solution)/shard_map/all_gather | solution.py:18
  626.7 1.9 fusion.24
  628.6 1.3 collective-permute-start.3
  629.9 3.4 collective-permute-done.3
  634.0 43.2 %all-gather.36.cloned.1.call-done = f32[1024,256]{1,0:T(8,128)} async-done(((f32[32,256]{1,0:T(8,128)}), f32[1024,256]{1,0:T(8,128)}) %all-gather.36.cloned.1.call-update) | async-done | bytes 1048592 | tf_op jit(solution)/shard_map/all_gather | solution.py:18
  677.2 2.5 broadcast_divide_fusion.2
  679.7 42.2 %all-gather.38.cloned.1.call-done = f32[1024,256]{1,0:T(8,128)} async-done(((f32[32,256]{1,0:T(8,128)}), f32[1024,256]{1,0:T(8,128)}) %all-gather.38.cloned.1.call-update) | async-done | bytes 1048592 | tf_op jit(solution)/shard_map/all_gather | solution.py:18
  722.0 2.5 fusion.20
  724.5 42.1 %all-gather.40.cloned.1.call-done = f32[1024,256]{1,0:T(8,128)} async-done(((f32[32,256]{1,0:T(8,128)}), f32[1024,256]{1,0:T(8,128)}) %all-gather.40.cloned.1.call-update) | async-done | bytes 1048592 | tf_op jit(solution)/shard_map/all_gather | solution.py:18
  766.7 1.9 fusion.17
  768.5 1.3 collective-permute-start.4
  769.8 3.4 collective-permute-done.4
  773.2 0.6 copy-done.11
  773.9 43.2 %all-gather.42.cloned.1.call-done = f32[1024,256]{1,0:T(8,128)} async-done(((f32[32,256]{1,0:T(8,128)}), f32[1024,256]{1,0:T(8,128)}) %all-gather.42.cloned.1.call-update) | async-done | bytes 1048592 | tf_op jit(solution)/shard_map/all_gather | solution.py:18
  817.1 2.5 broadcast_divide_fusion.1
  819.8 41.9 %all-gather.44.cloned.1.call-done = f32[1024,256]{1,0:T(8,128)} async-done(((f32[32,256]{1,0:T(8,128)}), f32[1024,256]{1,0:T(8,128)}) %all-gather.44.cloned.1.call-update) | async-done | bytes 1048592 | tf_op jit(solution)/shard_map/all_gather | solution.py:18
  861.8 2.5 fusion.13
  864.3 42.1 %all-gather.46.cloned.1.call-done = f32[1024,256]{1,0:T(8,128)} async-done(((f32[32,256]{1,0:T(8,128)}), f32[1024,256]{1,0:T(8,128)}) %all-gather.46.cloned.1.call-update) | async-done | bytes 1048592 | tf_op jit(solution)/shard_map/all_gather | solution.py:18
  906.4 1.9 fusion.10
  908.3 1.3 collective-permute-start.5
  909.6 3.4 collective-permute-done.5
  913.0 0.6 copy-done.12
  913.6 43.2 %all-gather.48.cloned.1.call-done = f32[1024,256]{1,0:T(8,128)} async-done(((f32[32,256]{1,0:T(8,128)}), f32[1024,256]{1,0:T(8,128)}) %all-gather.48.cloned.1.call-update) | async-done | bytes 1048592 | tf_op jit(solution)/shard_map/all_gather | solution.py:18
  956.8 2.5 broadcast_divide_fusion
  959.4 42.2 %all-gather.50.cloned.1.call-done = f32[1024,256]{1,0:T(8,128)} async-done(((f32[32,256]{1,0:T(8,128)}), f32[1024,256]{1,0:T(8,128)}) %all-gather.50.cloned.1.call-update) | async-done | bytes 1048592 | tf_op jit(solution)/shard_map/all_gather | solution.py:18
  1001.7 2.5 fusion.6
  1004.2 42.1 %all-gather.52.cloned.1.call-done = f32[1024,256]{1,0:T(8,128)} async-done(((f32[32,256]{1,0:T(8,128)}), f32[1024,256]{1,0:T(8,128)}) %all-gather.52.cloned.1.call-update) | async-done | bytes 1048592 | tf_op jit(solution)/shard_map/all_gather | solution.py:18
  1046.3 2.5 fusion.3
  1048.8 0.6 copy-done.13
  1049.6 41.5 %all-gather.54.cloned.1.call-done = f32[1024,256]{1,0:T(8,128)} async-done(((f32[32,256]{1,0:T(8,128)}), f32[1024,256]{1,0:T(8,128)}) %all-gather.54.cloned.1.call-update) | async-done | bytes 1048592 | tf_op jit(solution)/shard_map/all_gather | solution.py:91
  1091.1 45.4 %gather_fusion.1 = f32[1024]{0:T(1024)S(1)} fusion(f32[1024,256]{1,0:T(8,128)} %all-gather.54.cloned.1.call-done, s32[1024]{0:T(1024)S(1)} %bitcast.246), kind=kCustom, calls=%fused_computation.1 | custom fusion | bytes 16384 | tf_op jit(solution)/shard_map/jit(take_along_axis)/gather | solution.py:98
  1136.5 0.7 select_select_fusion
  (76 shorter events, 2.4 us)
Async XLA Ops:
  7.2 0.9 copy-start
  7.2 50.0 %all-gather.20.cloned.1.call-start = ((), (), s32[]{:S(2)}) async-start(), calls=%async_computation.3 | async-start | bytes 1081344 | tf_op jit(solution)/shard_map/all_gather | solution.py:18
  8.1 0.8 copy-start.2
  9.6 92.3 %all-gather.22.cloned.1.call-start = ((), (), s32[]{:S(2)}) async-start(), calls=%async_computation.4 | async-start | bytes 1081344 | tf_op jit(solution)/shard_map/all_gather | solution.py:18
  59.6 42.3 %copy-start.7 = (f32[32,256]{1,0:T(8,128)S(1)}, f32[32,256]{1,0:T(8,128)}, u32[]{:S(2)}) copy-start(f32[32,256]{1,0:T(8,128)} %fusion.45) | copy-start | bytes 98308
  59.7 44.2 %copy-start.1 = (f32[1,32,1024]{2,1,0:T(8,128)S(1)}, f32[1,32,1024]{2,1,0:T(8,128)}, u32[]{:S(2)}) copy-start(f32[1,32,1024]{2,1,0:T(8,128)} %param.21) | copy-start | bytes 393220
  59.7 121.4 %reduce-scatter.4.cloned.1.call-start = ((), (), s32[]{:S(2)}) async-start(), calls=%async_computation.5 | async-start | bytes 1081344 | tf_op jit(solution)/shard_map/reduce_scatter | solution.py:26
  105.9 126.2 %all-gather.24.cloned.1.call-start = ((), (), s32[]{:S(2)}) async-start(), calls=%async_computation.6 | async-start | bytes 1081344 | tf_op jit(solution)/shard_map/all_gather | solution.py:18
  181.1 4.4 collective-permute-start
  186.2 90.6 %all-gather.26.cloned.1.call-start = ((), (), s32[]{:S(2)}) async-start(), calls=%async_computation.7 | async-start | bytes 1081344 | tf_op jit(solution)/shard_map/all_gather | solution.py:18
  234.6 42.2 %copy-start.8 = (f32[32,256]{1,0:T(8,128)S(1)}, f32[32,256]{1,0:T(8,128)}, u32[]{:S(2)}) copy-start(f32[32,256]{1,0:T(8,128)} %fusion.39) | copy-start | bytes 98308
  234.6 121.2 %reduce-scatter.6.cloned.1.call-start = ((), (), s32[]{:S(2)}) async-start(), calls=%async_computation.8 | async-start | bytes 1081344 | tf_op jit(solution)/shard_map/reduce_scatter | solution.py:26
  280.7 126.2 %all-gather.28.cloned.1.call-start = ((), (), s32[]{:S(2)}) async-start(), calls=%async_computation.9 | async-start | bytes 1081344 | tf_op jit(solution)/shard_map/all_gather | solution.py:18
  355.9 4.4 collective-permute-start.1
  361.0 90.8 %all-gather.30.cloned.1.call-start = ((), (), s32[]{:S(2)}) async-start(), calls=%async_computation.10 | async-start | bytes 1081344 | tf_op jit(solution)/shard_map/all_gather | solution.py:18
  409.4 42.3 %copy-start.9 = (f32[32,256]{1,0:T(8,128)S(1)}, f32[32,256]{1,0:T(8,128)}, u32[]{:S(2)}) copy-start(f32[32,256]{1,0:T(8,128)} %fusion.33) | copy-start | bytes 98308
  409.5 121.4 %reduce-scatter.8.cloned.1.call-start = ((), (), s32[]{:S(2)}) async-start(), calls=%async_computation.11 | async-start | bytes 1081344 | tf_op jit(solution)/shard_map/reduce_scatter | solution.py:26
  455.7 126.2 %all-gather.32.cloned.1.call-start = ((), (), s32[]{:S(2)}) async-start(), calls=%async_computation.12 | async-start | bytes 1081344 | tf_op jit(solution)/shard_map/all_gather | solution.py:18
  530.9 4.4 collective-permute-start.2
  536.0 90.8 %all-gather.34.cloned.1.call-start = ((), (), s32[]{:S(2)}) async-start(), calls=%async_computation.13 | async-start | bytes 1081344 | tf_op jit(solution)/shard_map/all_gather | solution.py:18
  584.4 42.3 %copy-start.4 = (f32[32,256]{1,0:T(8,128)S(1)}, f32[32,256]{1,0:T(8,128)}, u32[]{:S(2)}) copy-start(f32[32,256]{1,0:T(8,128)} %fusion.27) | copy-start | bytes 98308
  584.4 92.7 %all-gather.36.cloned.1.call-start = ((), (), s32[]{:S(2)}) async-start(), calls=%async_computation.14 | async-start | bytes 1081344 | tf_op jit(solution)/shard_map/all_gather | solution.py:18
  628.6 4.7 collective-permute-start.3
  633.3 0.6 copy-start.10
  633.9 88.1 %all-gather.38.cloned.1.call-start = ((), (), s32[]{:S(2)}) async-start(), calls=%async_computation.15 | async-start | bytes 1081344 | tf_op jit(solution)/shard_map/all_gather | solution.py:18
  679.7 87.0 %all-gather.40.cloned.1.call-start = ((), (), s32[]{:S(2)}) async-start(), calls=%async_computation.16 | async-start | bytes 1081344 | tf_op jit(solution)/shard_map/all_gather | solution.py:18
  724.5 42.2 %copy-start.5 = (f32[32,256]{1,0:T(8,128)S(1)}, f32[32,256]{1,0:T(8,128)}, u32[]{:S(2)}) copy-start(f32[32,256]{1,0:T(8,128)} %fusion.20) | copy-start | bytes 98308
  724.5 92.6 %all-gather.42.cloned.1.call-start = ((), (), s32[]{:S(2)}) async-start(), calls=%async_computation.17 | async-start | bytes 1081344 | tf_op jit(solution)/shard_map/all_gather | solution.py:18
  768.5 4.7 collective-permute-start.4
  773.2 0.6 copy-start.11
  773.8 87.9 %all-gather.44.cloned.1.call-start = ((), (), s32[]{:S(2)}) async-start(), calls=%async_computation.18 | async-start | bytes 1081344 | tf_op jit(solution)/shard_map/all_gather | solution.py:18
  819.6 86.8 %all-gather.46.cloned.1.call-start = ((), (), s32[]{:S(2)}) async-start(), calls=%async_computation.19 | async-start | bytes 1081344 | tf_op jit(solution)/shard_map/all_gather | solution.py:18
  864.2 42.2 %copy-start.6 = (f32[32,256]{1,0:T(8,128)S(1)}, f32[32,256]{1,0:T(8,128)}, u32[]{:S(2)}) copy-start(f32[32,256]{1,0:T(8,128)} %fusion.13) | copy-start | bytes 98308
  864.3 92.6 %all-gather.48.cloned.1.call-start = ((), (), s32[]{:S(2)}) async-start(), calls=%async_computation.20 | async-start | bytes 1081344 | tf_op jit(solution)/shard_map/all_gather | solution.py:18
  908.3 4.7 collective-permute-start.5
  913.0 0.6 copy-start.12
  913.6 88.1 %all-gather.50.cloned.1.call-start = ((), (), s32[]{:S(2)}) async-start(), calls=%async_computation.21 | async-start | bytes 1081344 | tf_op jit(solution)/shard_map/all_gather | solution.py:18
  959.4 87.0 %all-gather.52.cloned.1.call-start = ((), (), s32[]{:S(2)}) async-start(), calls=%async_computation.22 | async-start | bytes 1081344 | tf_op jit(solution)/shard_map/all_gather | solution.py:18
  1004.1 42.2 %copy-start.3 = (f32[32,256]{1,0:T(8,128)S(1)}, f32[32,256]{1,0:T(8,128)}, u32[]{:S(2)}) copy-start(f32[32,256]{1,0:T(8,128)} %fusion.6) | copy-start | bytes 98308
  1004.2 87.0 %all-gather.54.cloned.1.call-start = ((), (), s32[]{:S(2)}) async-start(), calls=%async_computation.23 | async-start | bytes 1081344 | tf_op jit(solution)/shard_map/all_gather | solution.py:91
  1048.8 0.7 copy-start.13
Sparse Core Ops, SparseCore 0:
  10.8 46.2 all-gather.19
  60.0 41.9 all-gather.21
  106.0 74.9 reduce-scatter.3
  186.3 45.7 all-gather.23
  234.8 41.9 all-gather.25
  280.8 74.9 reduce-scatter.5
  361.1 45.7 all-gather.27
  409.8 41.9 all-gather.29
  455.8 74.9 reduce-scatter.7
  536.1 45.7 all-gather.31
  584.8 41.9 all-gather.33
  634.0 43.0 all-gather.35
  680.0 41.9 all-gather.37
  724.7 41.9 all-gather.39
  774.0 43.0 all-gather.41
  819.8 41.9 all-gather.43
  864.4 41.9 all-gather.45
  913.7 43.0 all-gather.47
  959.7 41.9 all-gather.49
  1004.3 41.9 all-gather.51
  1049.2 41.9 all-gather.53
where the time goes:
time: 1150 us; the launch traced here: 1140 us
  waiting for transfers between devices  1020 us (89%)
  local copies, waits for them, and re-layouts  49.6 us (4%)
  matrix products  44.8 us (4%)
  between operations  14.6 us (1%)
  starting transfers between devices  14.2 us (1%)
    all_gather x17, waiting for transfers between devices, product_rows(): shard_rows = lax.all_gather(panel_rows, 'panel', axis=0, tiled=True)  736 us
    reduce_scatter x3, waiting for transfers between devices, product_transposed(): lax.psum_scatter(lax.dot_general(matrix, panel_rows, (((0,), (0,)), ((),...  225 us
    gather x2, local copies, waits for them, and re-layouts, per_device(): taken = jnp.take_along_axis(shard_rows, where_rows, axis=1)  45.4 us
    all_gather x1, waiting for transfers between devices, per_device(): shard_rows = lax.all_gather(panels, 'panel', axis=1, tiled=True)  41.5 us
    dot_general x17, matrix products, product_rows(): jnp.dot(columns, shard_rows, precision=highest, preferred_element_type=jn...  38.7 us
  transfers between devices with their start and end apart: 27, of which 27 were waited for; matrix products, arithmetic and copies ran while one was open for 0% of the time, Pallas kernels for 0%

commit v1 on v0

--- a/solution.py
+++ b/solution.py
@@ -15,7 +15,10 @@
 
 def product_rows(matrix, panel_rows):
     initial = jnp.zeros((matrix.shape[0], panel_rows.shape[1]), jnp.float32)
-    shard_rows = lax.all_gather(panel_rows, "panel", axis=0, tiled=True)
+    n_dev = lax.axis_size("panel")
+    blocks = jnp.stack([panel_rows for _ in range(n_dev)])
+    blocks = lax.all_to_all(blocks, "panel", split_axis=0, concat_axis=0)
+    shard_rows = jnp.concatenate(blocks, axis=0)
     columns = lax.slice_in_dim(matrix, 0, shard_rows.shape[0], axis=1)
     return initial + jnp.dot(
         columns, shard_rows, precision=highest, preferred_element_type=jnp.float32

time: 1150 us -> 753 us (0.65)
  waiting for transfers between devices: 1020 us -> 296 us
  blocking collectives: 0 us -> 351 us
  matrix products: 44.8 us -> 17.7 us
    all_gather x17 -> x0, waiting for transfers between devices: 736 us -> none  [product_rows(): shard_rows = lax.all_gather(panel_rows, 'panel', axis=0, tiled=True)]
    all_to_all x0 -> x16, blocking collectives: none -> 351 us  [product_rows(): blocks = lax.all_to_all(blocks, 'panel', split_axis=0, concat_axis=0)]
    dot_general x17, matrix products: 38.7 us -> 11.7 us  [product_rows(): jnp.dot(columns, shard_rows, precision=highest, preferred_element_type=jn...]
    all_to_all x0 -> x1, waiting for transfers between devices: none -> 16.8 us  [product_rows(): blocks = lax.all_to_all(blocks, 'panel', split_axis=0, concat_axis=0)]
  transfers between devices with their start and end apart: 27 -> 11, of which waited for: 27 -> 11; matrix products, arithmetic and copies ran while one was open for 0% -> 0% of each run, Pallas kernels for 0% -> 0%
where the time goes in v1:
time: 753 us; the launch traced here: 748 us
  blocking collectives  351 us (47%)
  waiting for transfers between devices  296 us (39%)
  local copies, waits for them, and re-layouts  50.8 us (7%)
  matrix products  17.7 us (2%)
  starting transfers between devices  17.3 us (2%)
  between operations  14.2 us (2%)
    all_to_all x16, blocking collectives, product_rows(): blocks = lax.all_to_all(blocks, 'panel', split_axis=0, concat_axis=0)  351 us
    reduce_scatter x3, waiting for transfers between devices, product_transposed(): lax.psum_scatter(lax.dot_general(matrix, panel_rows, (((0,), (0,)), ((),...  223 us
    gather x2, local copies, waits for them, and re-layouts, per_device(): taken = jnp.take_along_axis(shard_rows, where_rows, axis=1)  45.4 us
    all_gather x1, waiting for transfers between devices, per_device(): shard_rows = lax.all_gather(panels, 'panel', axis=1, tiled=True)  40.5 us
    all_to_all x1, waiting for transfers between devices, product_rows(): blocks = lax.all_to_all(blocks, 'panel', split_axis=0, concat_axis=0)  16.8 us
    ppermute x6, waiting for transfers between devices, passed_along(): return lax.ppermute(block, axis, route)  16 us
  transfers between devices with their start and end apart: 11, of which 11 were waited for; matrix products, arithmetic and copies ran while one was open for 0% of the time, Pallas kernels for 0%

profile of v1, /device:TPU:1, one launch (start us, length us, event | category | flops | bytes accessed | tf_op | source)
XLA Modules:
  0.0 747.9 jit_solution(16065723720103580310)
XLA Ops:
  7.2 0.8 copy-done
  8.2 0.7 gather_fusion
  9.0 0.1 stack.37
  9.1 26.3 %all_to_all.86 = f32[32,32,256]{2,1,0:T(8,128)S(1)} all-to-all(f32[32,32,256]{2,1,0:T(8,128)S(1)} %stack.37), channel_id=1, replica_groups=mesh['depth'=4,'panel'=32] {'panel'}, dimensions={0} | all-to-all | bytes 2097152 | tf_op jit(solution)/shard_map/all_to_all | solution.py:20
  35.4 0.7 fusion.45
  36.2 20.6 %all_to_all.87 = f32[32,32,256]{2,1,0:T(8,128)S(1)} all-to-all(f32[32,32,256]{2,1,0:T(8,128)S(1)} %stack.38), channel_id=1, replica_groups=mesh['depth'=4,'panel'=32] {'panel'}, dimensions={0} | all-to-all | bytes 2097152 | tf_op jit(solution)/shard_map/all_to_all | solution.py:20
  56.8 0.7 fusion.42
  57.5 0.2 copy-done.1
  57.7 2.0 convolution_bitcast_fusion.2
  59.8 73.7 %reduce-scatter.4.cloned.1.call-done = f32[32,256]{1,0:T(8,128)} async-done(((f32[1024,256]{1,0:T(8,128)}), f32[32,256]{1,0:T(8,128)}) %reduce-scatter.4.cloned.1.call-update) | async-done | bytes 32784 | tf_op jit(solution)/shard_map/reduce_scatter | solution.py:29
  133.5 3.1 collective-permute-start
  136.6 1.3 collective-permute-done
  138.1 25.1 %all_to_all.88 = f32[32,32,256]{2,1,0:T(8,128)S(1)} all-to-all(f32[32,32,256]{2,1,0:T(8,128)S(1)} %stack.39), channel_id=1, replica_groups=mesh['depth'=4,'panel'=32] {'panel'}, dimensions={0} | all-to-all | bytes 2097152 | tf_op jit(solution)/shard_map/all_to_all | solution.py:20
  163.2 0.7 fusion.39
  164.0 20.6 %all_to_all.89 = f32[32,32,256]{2,1,0:T(8,128)S(1)} all-to-all(f32[32,32,256]{2,1,0:T(8,128)S(1)} %stack.40), channel_id=1, replica_groups=mesh['depth'=4,'panel'=32] {'panel'}, dimensions={0} | all-to-all | bytes 2097152 | tf_op jit(solution)/shard_map/all_to_all | solution.py:20
  184.7 0.7 fusion.36
  185.3 2.0 convolution_bitcast_fusion.1
  187.4 74.4 %reduce-scatter.6.cloned.1.call-done = f32[32,256]{1,0:T(8,128)} async-done(((f32[1024,256]{1,0:T(8,128)}), f32[32,256]{1,0:T(8,128)}) %reduce-scatter.6.cloned.1.call-update) | async-done | bytes 32784 | tf_op jit(solution)/shard_map/reduce_scatter | solution.py:29
  261.8 3.1 collective-permute-start.1
  264.9 1.3 collective-permute-done.1
  266.3 0.1 stack.41
  266.4 25.1 %all_to_all.90 = f32[32,32,256]{2,1,0:T(8,128)S(1)} all-to-all(f32[32,32,256]{2,1,0:T(8,128)S(1)} %stack.41), channel_id=1, replica_groups=mesh['depth'=4,'panel'=32] {'panel'}, dimensions={0} | all-to-all | bytes 2097152 | tf_op jit(solution)/shard_map/all_to_all | solution.py:20
  291.5 0.7 fusion.33
  292.3 20.6 %all_to_all.91 = f32[32,32,256]{2,1,0:T(8,128)S(1)} all-to-all(f32[32,32,256]{2,1,0:T(8,128)S(1)} %stack.42), channel_id=1, replica_groups=mesh['depth'=4,'panel'=32] {'panel'}, dimensions={0} | all-to-all | bytes 2097152 | tf_op jit(solution)/shard_map/all_to_all | solution.py:20
  312.9 0.7 fusion.30
  313.6 2.0 convolution_bitcast_fusion
  315.6 74.5 %reduce-scatter.8.cloned.1.call-done = f32[32,256]{1,0:T(8,128)} async-done(((f32[1024,256]{1,0:T(8,128)}), f32[32,256]{1,0:T(8,128)}) %reduce-scatter.8.cloned.1.call-update) | async-done | bytes 32784 | tf_op jit(solution)/shard_map/reduce_scatter | solution.py:29
  390.1 3.3 collective-permute-start.2
  393.4 0.1 fusion.52
  393.5 1.2 collective-permute-done.2
  394.9 24.9 %all_to_all.92 = f32[32,32,256]{2,1,0:T(8,128)S(1)} all-to-all(f32[32,32,256]{2,1,0:T(8,128)S(1)} %stack.43), channel_id=1, replica_groups=mesh['depth'=4,'panel'=32] {'panel'}, dimensions={0} | all-to-all | bytes 2097152 | tf_op jit(solution)/shard_map/all_to_all | solution.py:20
  419.8 0.7 fusion.27
  420.6 20.6 %all_to_all.93 = f32[32,32,256]{2,1,0:T(8,128)S(1)} all-to-all(f32[32,32,256]{2,1,0:T(8,128)S(1)} %stack.44), channel_id=1, replica_groups=mesh['depth'=4,'panel'=32] {'panel'}, dimensions={0} | all-to-all | bytes 2097152 | tf_op jit(solution)/shard_map/all_to_all | solution.py:20
  441.3 0.7 fusion.24
  441.9 1.3 collective-permute-start.3
  443.2 4.2 collective-permute-done.3
  447.5 21.2 %all_to_all.94 = f32[32,32,256]{2,1,0:T(8,128)S(1)} all-to-all(f32[32,32,256]{2,1,0:T(8,128)S(1)} %stack.45), channel_id=1, replica_groups=mesh['depth'=4,'panel'=32] {'panel'}, dimensions={0} | all-to-all | bytes 2097152 | tf_op jit(solution)/shard_map/all_to_all | solution.py:20
  468.7 0.7 broadcast_divide_fusion.2
  469.4 20.6 %all_to_all.95 = f32[32,32,256]{2,1,0:T(8,128)S(1)} all-to-all(f32[32,32,256]{2,1,0:T(8,128)S(1)} %stack.46), channel_id=1, replica_groups=mesh['depth'=4,'panel'=32] {'panel'}, dimensions={0} | all-to-all | bytes 2097152 | tf_op jit(solution)/shard_map/all_to_all | solution.py:20
  490.1 0.7 fusion.20
  490.9 20.6 %all_to_all.96 = f32[32,32,256]{2,1,0:T(8,128)S(1)} all-to-all(f32[32,32,256]{2,1,0:T(8,128)S(1)} %stack.47), channel_id=1, replica_groups=mesh['depth'=4,'panel'=32] {'panel'}, dimensions={0} | all-to-all | bytes 2097152 | tf_op jit(solution)/shard_map/all_to_all | solution.py:20
  511.5 0.7 fusion.17
  512.2 1.3 collective-permute-start.4
  513.5 4.0 collective-permute-done.4
  517.6 21.2 %all_to_all.97 = f32[32,32,256]{2,1,0:T(8,128)S(1)} all-to-all(f32[32,32,256]{2,1,0:T(8,128)S(1)} %stack.48), channel_id=1, replica_groups=mesh['depth'=4,'panel'=32] {'panel'}, dimensions={0} | all-to-all | bytes 2097152 | tf_op jit(solution)/shard_map/all_to_all | solution.py:20
  538.7 0.7 broadcast_divide_fusion.1
  539.5 20.6 %all_to_all.98 = f32[32,32,256]{2,1,0:T(8,128)S(1)} all-to-all(f32[32,32,256]{2,1,0:T(8,128)S(1)} %stack.49), channel_id=1, replica_groups=mesh['depth'=4,'panel'=32] {'panel'}, dimensions={0} | all-to-all | bytes 2097152 | tf_op jit(solution)/shard_map/all_to_all | solution.py:20
  560.1 0.7 fusion.13
  560.9 20.6 %all_to_all.99 = f32[32,32,256]{2,1,0:T(8,128)S(1)} all-to-all(f32[32,32,256]{2,1,0:T(8,128)S(1)} %stack.50), channel_id=1, replica_groups=mesh['depth'=4,'panel'=32] {'panel'}, dimensions={0} | all-to-all | bytes 2097152 | tf_op jit(solution)/shard_map/all_to_all | solution.py:20
  581.5 0.7 fusion.10
  582.2 1.3 collective-permute-start.5
  583.5 4.0 collective-permute-done.5
  587.6 21.2 %all_to_all.100 = f32[32,32,256]{2,1,0:T(8,128)S(1)} all-to-all(f32[32,32,256]{2,1,0:T(8,128)S(1)} %stack.51), channel_id=1, replica_groups=mesh['depth'=4,'panel'=32] {'panel'}, dimensions={0} | all-to-all | bytes 2097152 | tf_op jit(solution)/shard_map/all_to_all | solution.py:20
  608.8 0.7 broadcast_divide_fusion
  609.5 20.6 %all_to_all.101 = f32[32,32,256]{2,1,0:T(8,128)S(1)} all-to-all(f32[32,32,256]{2,1,0:T(8,128)S(1)} %stack.52), channel_id=1, replica_groups=mesh['depth'=4,'panel'=32] {'panel'}, dimensions={0} | all-to-all | bytes 2097152 | tf_op jit(solution)/shard_map/all_to_all | solution.py:20
  630.2 0.7 fusion.6
  630.8 1.1 stack.53
  631.9 3.9 all-to-all-start.16
  635.9 16.8 %all-to-all-done.16 = f32[32,32,256]{2,1,0:T(8,128)S(1)} async-done(((f32[32,32,256]{2,1,0:T(8,128)}), f32[32,32,256]{2,1,0:T(8,128)S(1)}, u32[]{:S(2)}, u32[]{:S(2)}) %all-to-all-start.16) | async-done | bytes 1048608 | tf_op jit(solution)/shard_map/all_to_all | solution.py:20
  652.8 1.3 fusion.3
  654.1 0.6 copy-done.3
  654.8 40.5 %all-gather.3.cloned.1.call-done = f32[1024,256]{1,0:T(8,128)} async-done(((f32[32,256]{1,0:T(8,128)}), f32[1024,256]{1,0:T(8,128)}) %all-gather.3.cloned.1.call-update) | async-done | bytes 1048592 | tf_op jit(solution)/shard_map/all_gather | solution.py:94
  695.3 45.4 %gather_fusion.1 = f32[1024]{0:T(1024)S(1)} fusion(f32[1024,256]{1,0:T(8,128)} %all-gather.3.cloned.1.call-done, s32[1024]{0:T(1024)S(1)} %bitcast.265), kind=kCustom, calls=%fused_computation.1 | custom fusion | bytes 16384 | tf_op jit(solution)/shard_map/jit(take_along_axis)/gather | solution.py:101
  740.7 0.7 select_select_fusion
  (40 shorter events, 2.3 us)
Async XLA Ops:
  7.2 0.9 copy-start
  7.2 126.4 %reduce-scatter.4.cloned.1.call-start = ((), (), s32[]{:S(2)}) async-start(), calls=%async_computation.20 | async-start | bytes 1081344 | tf_op jit(solution)/shard_map/reduce_scatter | solution.py:29
  8.1 0.8 copy-start.2
  56.8 0.9 copy-start.1
  59.7 202.1 %reduce-scatter.6.cloned.1.call-start = ((), (), s32[]{:S(2)}) async-start(), calls=%async_computation.21 | async-start | bytes 1081344 | tf_op jit(solution)/shard_map/reduce_scatter | solution.py:29
  133.5 4.4 collective-permute-start
  187.4 202.8 %reduce-scatter.8.cloned.1.call-start = ((), (), s32[]{:S(2)}) async-start(), calls=%async_computation.22 | async-start | bytes 1081344 | tf_op jit(solution)/shard_map/reduce_scatter | solution.py:29
  261.8 4.4 collective-permute-start.1
  390.1 4.6 collective-permute-start.2
  441.9 5.5 collective-permute-start.3
  512.2 5.3 collective-permute-start.4
  582.2 5.3 collective-permute-start.5
  631.9 20.8 %all-to-all-start.16 = ((f32[32,32,256]{2,1,0:T(8,128)}), f32[32,32,256]{2,1,0:T(8,128)S(1)}, u32[]{:S(2)}, u32[]{:S(2)}) async-start(f32[32,32,256]{2,1,0:T(8,128)} %stack.53), calls=%async_computation.19 | async-start | bytes 2097152 | tf_op jit(solution)/shard_map/all_to_all | solution.py:20
  635.9 59.5 %all-gather.3.cloned.1.call-start = ((), (), s32[]{:S(2)}) async-start(), calls=%async_computation.23 | async-start | bytes 1081344 | tf_op jit(solution)/shard_map/all_gather | solution.py:94
  654.0 0.7 copy-start.3
Sparse Core Ops, SparseCore 0:
  59.9 73.6 reduce-scatter.3
  187.5 74.2 reduce-scatter.5
  315.7 74.3 reduce-scatter.7
  654.2 41.1 all-gather.2
